TPU v7x, 32 devices: a whole 2x2x4 slice. The times are simulated.
32 devices in a mesh: sec: 4 (over y, core), dev: 8 (over z, x).
Axes of the slice: x: 2, y: 2, z: 4, core: 2. Of those that a mesh axis runs over, the one named last changes fastest.
Arguments:
- potential: float32 [64, 32, 512], P('dev', None, 'sec'), may hold values from -6 to 6
- previous: float32 [64, 32, 512], P('dev', None, 'sec'), may hold values from -6 to 6
- wave_coeff: float32 [64, 32, 512], P('dev', None, 'sec'), may hold values from 0.03 to 0.16
- sketch_in: bfloat16 [16384, 512], P('dev'), may hold values from -6 to 6
- omega: float32 [64, 512], replicated, may hold values from -6 to 6
- blocks: int32 [8, 9], P('dev'), may hold values from 0 to 255, as said below
- owners: int32 [8, 9], P('dev'), may hold values from 0 to 7, as said below
Outputs:
- basis: bfloat16 [4, 16384, 512], P('sec', 'dev')
- gram_factor: float32 [4, 512, 512], P('sec')
Inputs may be any that keep to these rules, and one draw needn't show every extreme that they name: `blocks`: within one section's 3 entries of a row the block numbers are distinct. Within a row of owners no owner appears more than 2 times, and one owner, the same for all rows, appears exactly 2 times in every row.
All inputs are finite; a program needn't handle non-finite values.
Results may differ from a plain program's by a relative error of at most 0.003.
Values sent between devices are 32-bit elements; how exact they have to be, the bound alone decides.
No kernel may reach another device: no remote copies, remote signals or barrier semaphores. Data moves between devices by JAX's collectives and lax.ppermute only.
A program may use at most 256 MiB of HBM per device.

v0:
```python
import functools
import math

import jax
import jax.numpy as jnp
import numpy as np
from jax import lax
from jax.experimental import pallas as pl
from jax.experimental.pallas import tpu as pltpu
from jax.sharding import PartitionSpec as P

CAP = 2
damping = 0.05
LANES = 128
highest = lax.Precision.HIGHEST
decay = math.sqrt(1.0 - damping)
BOTH = ("sec", "dev")


def neighbour_path(columns):
    order = []
    for i in range(0, columns, 2):
        pair = [i, i + 1]
        order += pair if (i // 2) % 2 == 0 else pair[::-1]
    return order


def vmem(*arrays):
    return [pl.BlockSpec(memory_space=pltpu.VMEM)] * len(arrays)


def big(limit=48):
    return pltpu.CompilerParams(vmem_limit_bytes=limit << 20)


def slab_of(order, column, section, per_slab):
    place = order.index(column)
    forward, backward = place // per_slab, (len(order) - 1 - place) // per_slab
    return jnp.where(section % 2 == 0, forward, backward)


def split_kernel(order, slab, per_slab, u_ref, e_ref, k_ref, table_ref, out_ref, turned):
    section = lax.axis_index("sec")
    extent_x, extent_y, depth = u_ref.shape
    for a, ref in enumerate((u_ref, e_ref, k_ref)):
        for p in range(2):
            rows = jnp.concatenate([ref[x] for x in range(p, extent_x, 2)], axis=0)
            if a == 1:
                rows = rows * decay
            turned[2 * a + p] = rows.T
    for column in range(len(order)):
        at = slab_of(order, column, section, per_slab)
        start = pl.multiple_of(at * slab, 8)
        for q in range(6):
            out_ref[column, q * slab : (q + 1) * slab, :] = turned[q, pl.ds(start, slab), :]
        out_ref[column, 6 * slab :, :] = jnp.broadcast_to(table_ref[...], (8, LANES))


def steps_kernel(*args):
    sections = args[5]

    @pl.when(lax.axis_index("sec") < sections - 1)
    def _():
        evolve(*args)


def evolve(
    first_step, slab, per_device, last, snaps, sections,
    table, kl, kc, kr, sl, sc, sr, w_in, *rest,
):
    if last:
        send_ref, w_ref, field_a, field_b, gain, own = rest
    else:
        state_ref, w_ref, field_a, field_b, gain, own = rest
    list_start = lax.axis_index("sec") * per_device
    columns = kc.shape[0]
    rows = 3 * slab
    lane = lax.broadcasted_iota(jnp.int32, (8, LANES), 1)
    y_first, y_last = lane % 32 == 0, lane % 32 == 31
    zero = jnp.zeros((8, LANES), jnp.float32)

    for o in range(2 * columns):
        d, p = o // 2, o % 2
        for field, at in ((field_a, p), (field_b, 2 + p)):
            field[o, 0:8, :] = zero
            field[o, 8 + rows : 16 + rows, :] = zero
            for h, ref in enumerate((sl, sc, sr)):
                field[o, 8 + h * slab : 8 + (h + 1) * slab, :] = ref[
                    d, at * slab : (at + 1) * slab, :
                ]
        for h, ref in enumerate((kl, kc, kr)):
            k = ref[d, (4 + p) * slab : (5 + p) * slab, :]
            gain[o, h * slab : (h + 1) * slab, :] = k * (1.0 / decay)
            own[o, h * slab : (h + 1) * slab, :] = ((2.0 - damping) - 6.0 * k) * (1.0 / decay)
    w_ref[...] = w_in[...]

    def step(src, dst, tiles, number):
        for z in tiles:
            at = slice(8 + 8 * z, 16 + 8 * z)
            low = slice(7 + 8 * z, 15 + 8 * z)
            high = slice(9 + 8 * z, 17 + 8 * z)
            here = slice(8 * z, 8 * z + 8)
            values = [src[o, at, :] for o in range(2 * columns)]
            up = [pltpu.roll(values[2 * d + 1], 32, 1) for d in range(columns)]
            down = [pltpu.roll(values[2 * d], LANES - 32, 1) for d in range(columns)]
            for o in range(2 * columns):
                d, p = o // 2, o % 2
                v = values[o]
                if p == 0:
                    side = jnp.where(lane < 32, up[d - 1] if d > 0 else zero, up[d])
                    total = values[o + 1] + side
                else:
                    side = jnp.where(
                        lane >= LANES - 32, down[d + 1] if d + 1 < columns else zero, down[d]
                    )
                    total = values[o - 1] + side
                total = total + (src[o, low, :] + src[o, high, :])
                total = total + jnp.where(y_first, 0.0, pltpu.roll(v, 1, 1))
                total = total + jnp.where(y_last, 0.0, pltpu.roll(v, LANES - 1, 1))
                dst[o, at, :] = own[o, here, :] * v + gain[o, here, :] * total - dst[o, at, :]

        def column_blocks(d, carry):
            for i in range(per_device):
                block = table[d, list_start + i]
                x, y = block >> 5, block & 31
                at_lane = ((x >> 1) << 5) + y
                o = 2 * d + (x & 1)
                j = d * per_device + i
                held = w_ref[j]
                for h in range(slab // 8):
                    target = h * snaps + number
                    value = dst[o, 8 + slab + 8 * h : 16 + slab + 8 * h, :]
                    moved = pltpu.roll(value, (target - at_lane) & (LANES - 1), 1)
                    held = jnp.where(lane == target, moved, held)
                w_ref[j] = held
            return carry

        lax.fori_loop(0, columns, column_blocks, 0, unroll=min(columns, 8))

    for phase in range(slab // 8):
        tiles = range(phase, 3 * slab // 8 - phase)

        def pair(m, carry):
            number = first_step + 8 * phase + 2 * m
            step(field_a, field_b, tiles, number)
            step(field_b, field_a, tiles, number + 1)
            return carry

        lax.fori_loop(0, 4, pair, 0)

    if last:
        send_ref[...] = jnp.zeros(send_ref.shape, jnp.float32)
        width = per_device * (sections - 1)

        def place(d, carry):
            for i in range(per_device):
                mine = table[d, width + list_start + i]

                def earlier(n, c):
                    return c + jnp.where(table[d, width + n] == mine, 1, 0)

                count = lax.fori_loop(0, list_start + i, earlier, 0)
                send_ref[mine, d * CAP + count] = w_ref[d * per_device + i]
            return carry

        lax.fori_loop(0, columns, place, 0)
    else:
        for o in range(2 * columns):
            d, p = o // 2, o % 2
            state_ref[d, p * slab : (p + 1) * slab, :] = field_a[o, 8 + slab : 8 + 2 * slab, :]
            state_ref[d, (2 + p) * slab : (3 + p) * slab, :] = field_b[
                o, 8 + slab : 8 + 2 * slab, :
            ]


def unpack(tile, h, snaps, lane):
    if h:
        tile = pltpu.roll(tile, LANES - h * snaps, 1)
    return jnp.where(lane < snaps, tile, 0.0)


def product_kernel(*args):
    sections = args[4]

    @pl.when(lax.axis_index("sec") < sections - 1)
    def _():
        products(*args)


def products(order, slab, per_slab, snaps, sections, w_ref, s_ref, out_ref, wide, low):
    section = lax.axis_index("sec")
    slots = w_ref.shape[1]
    halves = slab // 8
    lane = lax.broadcasted_iota(jnp.int32, (8, LANES), 1)
    for column in range(0, len(order)):
        if order.index(column) % per_slab:
            continue
        at = slab_of(order, column, section, per_slab)
        for q in range(slots):
            tile = w_ref[column, q]
            for h in range(halves):
                w = unpack(tile, h, snaps, lane)
                w1 = w.astype(jnp.bfloat16).astype(jnp.float32)
                w2 = (w - w1).astype(jnp.bfloat16).astype(jnp.float32)
                w3 = w - w1 - w2
                start = pl.multiple_of(q * LANES + at * slab + 8 * h, 8)
                wide[pl.ds(start, 8), :] = w1 + pltpu.roll(w2, snaps, 1)
                low[pl.ds(start, 8), :] = w3
    both = wide[...].astype(jnp.bfloat16)
    tail = low[...].astype(jnp.bfloat16)
    rows = (((0,), (0,)), ((), ()))
    dot = functools.partial(
        lax.dot_general, dimension_numbers=rows, preferred_element_type=jnp.float32
    )
    sketch = s_ref[...]
    a_first = dot(both, sketch)
    a_tail = dot(tail, sketch)
    cross = a_first[:snaps] + (a_first[snaps:] + a_tail[:snaps])
    c_first = dot(both, both)
    c_tail = dot(tail, both)[:snaps, :]
    c_tail = jnp.where(lax.broadcasted_iota(jnp.int32, c_tail.shape, 1) < snaps, c_tail, 0.0)
    half = c_first[:snaps, :] + c_first[snaps:, :]
    own = half + pltpu.roll(half, snaps, 1)
    square = jnp.concatenate([c_tail, jnp.zeros_like(c_tail)], axis=0).T[:snaps, :]
    inner = jnp.where(
        lax.broadcasted_iota(jnp.int32, own.shape, 1) < snaps, own, 0.0
    ) + (c_tail + square)
    strips = cross.shape[1] // LANES
    share = out_ref.shape[1]
    for r in range(snaps // 8):
        here = slice(8 * r, 8 * r + 8)
        for c in range(strips):
            at = r * (strips + 1) + c
            out_ref[at // share, at % share] = cross[here, c * LANES : (c + 1) * LANES]
        at = r * (strips + 1) + strips
        out_ref[at // share, at % share] = inner[here, :]


def three(x):
    x1 = x.astype(jnp.bfloat16)
    rest = x - x1.astype(jnp.float32)
    x2 = rest.astype(jnp.bfloat16)
    return x1, x2, (rest - x2.astype(jnp.float32)).astype(jnp.bfloat16)


def factor_block(d, e, sub, lane):
    tiles = len(d)

    def wide(x):
        return jnp.broadcast_to(x, (8, LANES))

    def stack(values):
        out = values[0]
        for j in range(1, 8):
            out = jnp.where(sub == j, values[j], out)
        return out

    for p in range(tiles):
        first = 8 * p
        cols = [wide(d[p][:, first + j : first + j + 1]) for j in range(8)]
        s = [[wide(cols[k][j : j + 1, :]) if k >= j else None for k in range(8)] for j in range(8)]
        t = [wide(d[p][j : j + 1, :]) for j in range(8)]
        te = [wide(e[p][j : j + 1, :]) for j in range(8)]
        inv, m = [], [[None] * 8 for _ in range(8)]
        for j in range(8):
            guess = pl.reciprocal(s[j][j], approx=True)
            guess = guess * (2.0 - s[j][j] * guess)
            inv.append(guess * (2.0 - s[j][j] * guess))
            for k in range(j + 1, 8):
                m[j][k] = s[j][k] * inv[j]
            for k in range(j + 1, 8):
                for n in range(k, 8):
                    s[k][n] = s[k][n] - m[j][k] * s[j][n]
                t[k] = t[k] - m[j][k] * t[j]
                te[k] = te[k] - m[j][k] * te[j]
        if p + 1 < tiles:
            z, ze = [None] * 8, [None] * 8
            for j in reversed(range(8)):
                z[j], ze[j] = t[j] * inv[j], te[j] * inv[j]
                for k in range(j + 1, 8):
                    z[j] = z[j] - m[j][k] * z[k]
                    ze[j] = ze[j] - m[j][k] * ze[k]
            i = p + 1
            parts, parts_e = [], []
            for j in range(8):
                col = wide(d[i][:, first + j : first + j + 1])
                parts.append(col * z[j])
                parts_e.append(col * ze[j])
            while len(parts) > 1:
                parts = [x + y for x, y in zip(parts[::2], parts[1::2])]
                parts_e = [x + y for x, y in zip(parts_e[::2], parts_e[1::2])]
            if p + 2 < tiles:
                p1, p2, p3 = three(d[p])
                z1, z2, z3 = three(jnp.concatenate([stack(z), stack(ze)], axis=1))
                change = lax.dot_general(
                    jnp.concatenate([p1, p1, p1, p2, p2, p3], axis=0),
                    jnp.concatenate([z1, z2, z3, z1, z2, z1], axis=0),
                    (((0,), (0,)), ((), ())),
                    preferred_element_type=jnp.float32,
                )
                for n in range(p + 2, tiles):
                    d[n] = d[n] - change[8 * n : 8 * n + 8, :LANES]
                    e[n] = e[n] - change[8 * n : 8 * n + 8, LANES:]
            d[i], e[i] = d[i] - parts[0], e[i] - parts_e[0]
        roots = [lax.rsqrt(s[j][j]) for j in range(8)]
        d[p] = jnp.where(lane >= sub + first, stack([t[j] * roots[j] for j in range(8)]), 0.0)
        e[p] = stack([te[j] * roots[j] for j in range(8)])
    return jnp.concatenate(d, axis=0), jnp.concatenate(e, axis=0)


def factor_kernel(scale, sections, parts_ref, omega_ref, s_ref, factor_ref, inverse_ref, g):
    analysis = lax.axis_index("sec") == sections - 1

    @pl.when(analysis)
    def _():
        factorize(scale, parts_ref, omega_ref, s_ref, factor_ref, inverse_ref, g)

    @pl.when(jnp.logical_not(analysis))
    def _():
        factor_ref[...] = jnp.zeros(factor_ref.shape, jnp.float32)


def factorize(scale, parts_ref, omega_ref, s_ref, factor_ref, inverse_ref, g):
    rank = s_ref.shape[0]
    snaps = omega_ref.shape[0]
    strips = rank // LANES
    rows_first = (((0,), (0,)), ((), ()))

    def band(r, c):
        return parts_ref[r * (strips + 1) + c]

    cross = jnp.concatenate(
        [
            jnp.concatenate([band(r, c) for c in range(strips)], axis=1)
            for r in range(snaps // 8)
        ],
        axis=0,
    )
    inner = jnp.concatenate([band(r, strips) for r in range(snaps // 8)], axis=0)
    omega = omega_ref[...]
    half = cross + 0.5 * jnp.dot(
        inner[:, :snaps], omega, precision=highest, preferred_element_type=jnp.float32
    )
    left = jnp.concatenate([half, omega], axis=0)
    right = jnp.concatenate([omega, half], axis=0)
    g[...] = s_ref[...] + lax.dot_general(
        left, right, rows_first, precision=highest, preferred_element_type=jnp.float32
    )
    inverse_ref[...] = jnp.zeros(inverse_ref.shape, jnp.float32)
    factor_ref[...] = jnp.zeros(factor_ref.shape, jnp.float32)
    sub = lax.broadcasted_iota(jnp.int32, (8, LANES), 0)
    lane = lax.broadcasted_iota(jnp.int32, (8, LANES), 1)
    tiles = LANES // 8

    def block(k, carry):
        start = pl.multiple_of(k * LANES, LANES)
        d = [g[pl.ds(start + 8 * i, 8), pl.ds(start, LANES)] for i in range(tiles)]
        e = [jnp.where(lane == sub + 8 * i, 1.0, 0.0) for i in range(tiles)]
        upper, small = factor_block(d, e, sub, lane)
        factor_ref[pl.ds(start, LANES), pl.ds(start, LANES)] = upper
        inverse_ref[pl.ds(start, LANES), pl.ds(start, LANES)] = small
        for at in range(strips):

            @pl.when(k == at)
            def _(at=at):
                rows = slice(at * LANES, (at + 1) * LANES)
                right, left = slice((at + 1) * LANES, rank), slice(0, at * LANES)
                ahead = rank - (at + 1) * LANES
                pieces = [g[rows, right]] if ahead else []
                pieces += [inverse_ref[rows, left]] if at else []
                panel = jnp.dot(
                    small,
                    jnp.concatenate(pieces, axis=1),
                    precision=highest,
                    preferred_element_type=jnp.float32,
                )
                if at:
                    inverse_ref[rows, left] = panel[:, ahead:]
                if ahead:
                    fresh = panel[:, :ahead]
                    factor_ref[rows, right] = fresh
                    change = lax.dot_general(
                        fresh,
                        jnp.concatenate([panel, small], axis=1),
                        rows_first,
                        precision=highest,
                        preferred_element_type=jnp.float32,
                    )
                    g[right, right] = g[right, right] - change[:, :ahead]
                    done = slice(0, (at + 1) * LANES)
                    inverse_ref[right, done] = inverse_ref[right, done] - change[:, ahead:]

        return carry

    lax.fori_loop(0, strips, block, 0)
    factor_ref[...] = factor_ref[...] * (1.0 / scale)
    inverse_ref[...] = (inverse_ref[...] * scale).T


def basis_kernel(sections, inverse_ref, omega_ref, s_ref, *rest):
    pieces, out_ref = rest[:-1], rest[-1]
    analysis = lax.axis_index("sec") == sections - 1

    @pl.when(analysis)
    def _():
        def split(x):
            high = x.astype(jnp.bfloat16)
            return high, (x - high.astype(jnp.float32)).astype(jnp.bfloat16)

        dot = functools.partial(jnp.dot, preferred_element_type=jnp.float32)
        inverse = inverse_ref[...]
        mixed = jnp.dot(
            omega_ref[...], inverse, precision=highest, preferred_element_type=jnp.float32
        )
        x1, x2 = split(inverse)
        m1, m2 = split(jnp.concatenate([mixed, mixed], axis=0))
        rows = 512

        def strip(i, carry):
            at = pl.ds(pl.multiple_of(i * rows, rows), rows)
            s = s_ref[at, :]
            w = pieces[0][at, :]
            for piece in pieces[1:]:
                w = w + piece[at, :]
            w = w.astype(jnp.bfloat16)
            q = (dot(s, x1) + dot(s, x2)) + (dot(w, m1) + dot(w, m2))
            out_ref[at, :] = q.astype(jnp.bfloat16)
            return carry

        lax.fori_loop(0, s_ref.shape[0] // rows, strip, 0)

    @pl.when(jnp.logical_not(analysis))
    def _():
        out_ref[...] = jnp.zeros(out_ref.shape, jnp.bfloat16)


def shards(potential, previous, wave_coeff, sketch_in, omega, blocks, owners):
    sections = lax.axis_size("sec")
    columns = lax.axis_size("dev")
    devices = sections * columns
    extent_x, extent_y, depth = potential.shape
    list_width = owners.shape[1]
    per_device = list_width // (sections - 1)
    snaps, rank = omega.shape
    slab = max(8, depth // columns)
    per_slab = slab * columns // depth
    slots = columns * CAP
    order = neighbour_path(columns)
    path = []
    for section in range(sections - 1):
        path += [section * columns + d for d in (order if section % 2 == 0 else order[::-1])]
    up = [(path[i], path[i + per_slab]) for i in range(len(path) - per_slab)]
    down = [(b, a) for a, b in up]
    f32 = jnp.float32

    analysis = lax.axis_index("sec") == sections - 1

    def whole_gram():
        own = lax.dot_general(
            sketch_in, sketch_in, (((0,), (0,)), ((), ())), preferred_element_type=f32
        )
        own = own.reshape(columns, rank // columns, rank)
        own = lax.all_to_all(own, "dev", split_axis=0, concat_axis=0, tiled=True)
        own = jnp.broadcast_to(jnp.sum(own, axis=0)[None], own.shape)
        own = lax.all_to_all(own, "dev", split_axis=0, concat_axis=0, tiled=True)
        return own.reshape(rank, rank)

    scaled = omega * jnp.asarray(
        decay ** np.arange(1, snaps + 1, dtype=np.float64), f32
    )[:, None]

    lists = jnp.pad(
        jnp.concatenate([blocks, owners], axis=1).astype(f32), ((0, 0), (0, LANES - 2 * list_width))
    )
    chunk = 6 * slab + 8
    operands = (potential, previous, wave_coeff, lists)
    outgoing = pl.pallas_call(
        functools.partial(split_kernel, order, slab, per_slab),
        out_shape=jax.ShapeDtypeStruct((columns, chunk, LANES), f32),
        in_specs=vmem(*operands),
        out_specs=pl.BlockSpec(memory_space=pltpu.VMEM),
        scratch_shapes=[pltpu.VMEM((6, depth, LANES), f32)],
        compiler_params=big(),
    )(*operands)
    raw = lax.all_to_all(outgoing, "dev", split_axis=0, concat_axis=0, tiled=True)
    gram, scaled, raw = lax.optimization_barrier(
        (lax.cond(analysis, whole_gram, lambda: jnp.zeros((rank, rank), f32)), scaled, raw)
    )
    table = raw[:, 6 * slab, : 2 * list_width].astype(jnp.int32)

    def sides(x):
        return lax.ppermute(x, BOTH, up), x, lax.ppermute(x, BOTH, down)

    fields = sides(raw)
    state = fields
    held = jnp.zeros((columns * per_device, 8, LANES), f32)
    rounds = snaps // slab
    for number in range(rounds):
        last = number == rounds - 1
        operands = (table, *fields, *state, held)
        result = (columns, slots, 8, LANES) if last else (columns, 4 * slab, LANES)
        moved, held = pl.pallas_call(
            functools.partial(
                steps_kernel, number * slab, slab, per_device, last, snaps, sections
            ),
            out_shape=(
                jax.ShapeDtypeStruct(result, f32),
                jax.ShapeDtypeStruct(held.shape, f32),
            ),
            in_specs=[pl.BlockSpec(memory_space=pltpu.SMEM)] + vmem(*operands[1:]),
            out_specs=tuple(vmem(0, 0)),
            scratch_shapes=[pltpu.VMEM((2 * columns, 3 * slab + 16, LANES), f32)] * 2
            + [pltpu.VMEM((2 * columns, 3 * slab, LANES), f32)] * 2,
            compiler_params=big(),
        )(*operands)
        if not last:
            state = sides(moved)
    arrived = lax.all_to_all(moved, "dev", split_axis=0, concat_axis=0, tiled=True)

    operands = (arrived, sketch_in)
    bands = (snaps // 8) * (rank // LANES + 1)
    share = -(-bands // columns)
    parts, wide = pl.pallas_call(
        functools.partial(product_kernel, order, slab, per_slab, snaps, sections),
        out_shape=(
            jax.ShapeDtypeStruct((columns, share, 8, LANES), f32),
            jax.ShapeDtypeStruct((slots * depth, LANES), f32),
        ),
        in_specs=vmem(*operands),
        out_specs=tuple(vmem(0, 0)),
        scratch_shapes=[pltpu.VMEM((slots * depth, LANES), f32)],
        compiler_params=big(60),
    )(*operands)

    def to_analysis(x):
        return [lax.ppermute(x, "sec", [(i, sections - 1)]) for i in range(sections - 1)]

    terms = lax.all_to_all(parts, "dev", split_axis=0, concat_axis=0, tiled=True)
    terms = to_analysis(jnp.sum(terms, axis=0))
    hop = lax.ppermute(wide, "sec", [(i, i + 1) for i in range(0, sections - 1, 2)])
    merged, terms = lax.optimization_barrier((wide + hop, terms))
    pieces = [hop]
    pieces += [lax.ppermute(merged, "sec", [(i, sections - 1)]) for i in range(1, sections - 1, 2)]

    def exchange(terms):
        total = jnp.broadcast_to(sum(terms[1:], terms[0])[None], parts.shape)
        return lax.all_to_all(total, "dev", split_axis=0, concat_axis=0, tiled=True)

    sums = lax.cond(analysis, exchange, lambda terms: jnp.zeros(parts.shape, f32), terms)
    sums = sums.reshape(columns * share, 8, LANES)

    scale = math.sqrt(columns * columns * CAP * depth)
    operands = (sums, scaled, gram)
    factor, inverse = pl.pallas_call(
        functools.partial(factor_kernel, scale, sections),
        out_shape=(jax.ShapeDtypeStruct((rank, rank), f32),) * 2,
        in_specs=vmem(*operands),
        out_specs=tuple(vmem(0, 0)),
        scratch_shapes=[pltpu.VMEM((rank, rank), f32)],
        compiler_params=big(),
    )(*operands)
    operands = (inverse, scaled, sketch_in, *pieces)
    basis = pl.pallas_call(
        functools.partial(basis_kernel, sections),
        out_shape=jax.ShapeDtypeStruct(sketch_in.shape, jnp.bfloat16),
        in_specs=vmem(*operands),
        out_specs=pl.BlockSpec(memory_space=pltpu.VMEM),
        compiler_params=big(60),
    )(*operands)
    return (basis[None], factor[None])


def solution(mesh):
    placed = (
        P("dev", None, "sec"),
        P("dev", None, "sec"),
        P("dev", None, "sec"),
        P("dev", None),
        P(),
        P("dev", None),
        P("dev", None),
    )
    return jax.shard_map(
        shards,
        mesh=mesh,
        in_specs=placed,
        out_specs=(P("sec", "dev", None), P("sec", None, None)),
        check_vma=False,
    )
```

profile of v0, /device:TPU:5, one launch (start us, length us, event | category | flops | bytes accessed | tf_op | source)
XLA Modules:
  0.0 190.3 jit_solution(15667018098261046417)
XLA Ops:
  0.6 0.7 add_convert_fusion
  1.4 46.4 %conditional.2 = (f32[512,512]{1,0:T(8,128)S(1)}) conditional(s32[]{:T(128)} %convert_element_type.22, () %tuple.25, bf16[2048,512]{1,0:T(8,128)(2,1)} %s_ref.1), branch_computations={%region_0.1_spmd, %region_1.3_spmd} | conditional | flops 1073971200 | bytes 9699340 | solution.py:487
  1.5 3.6 %fusion = f32[512,512]{1,0:T(8,128)S(1)} fusion(bf16[2048,512]{1,0:T(8,128)(2,1)} %param.1), kind=kOutput, calls=%fused_computation.4 | convolution fusion | flops 1073741824 | bytes 3145728 | tf_op jit(solution)/shard_map/cond/branch_1_fun/dot_general | solution.py:459
  5.1 24.8 %all_to_all.27 = f32[8,64,512]{2,1,0:T(8,128)S(1)} all-to-all(f32[8,64,512]{2,1,0:T(8,128)S(1)} %bitcast.14), channel_id=1, replica_groups=mesh['sec'=4,'dev'=8] {'dev'}, dimensions={0} | all-to-all | bytes 2097152 | tf_op jit(solution)/shard_map/cond/branch_1_fun/all_to_all | solution.py:463
  30.1 17.7 %all_to_all.28 = f32[8,64,512]{2,1,0:T(8,128)S(1)} all-to-all(f32[8,64,512]{2,1,0:T(8,128)S(1)} %broadcast_in_dim.5), channel_id=1, replica_groups=mesh['sec'=4,'dev'=8] {'dev'}, dimensions={0} | all-to-all | bytes 2097152 | tf_op jit(solution)/shard_map/cond/branch_1_fun/all_to_all | solution.py:465
  47.8 1.1 shard_map.98
  48.9 3.7 %all-to-all-start.3 = ((f32[8,104,128]{2,1,0:T(8,128)}), f32[8,104,128]{2,1,0:T(8,128)S(1)}, u32[]{:S(2)}, u32[]{:S(2)}) async-start(f32[8,104,128]{2,1,0:T(8,128)} %shard_map.98), calls=%async_computation.3 | async-start | bytes 851968 | tf_op jit(solution)/shard_map/all_to_all | solution.py:485
  52.8 9.4 %all-to-all-done.3.args_2_.args_5_ = f32[8,104,128]{2,1,0:T(8,128)S(1)} async-done(((f32[8,104,128]{2,1,0:T(8,128)}), f32[8,104,128]{2,1,0:T(8,128)S(1)}, u32[]{:S(2)}, u32[]{:S(2)}) %all-to-all-start.3) | async-done | bytes 426016 | tf_op jit(solution)/shard_map/all_to_all | solution.py:485
  62.8 0.7 collective-permute-start
  64.2 0.7 collective-permute-start.3
  64.9 0.7 collective-permute-start.2
  66.2 0.7 collective-permute-start.5
  66.9 0.7 collective-permute-start.4
  68.2 0.8 collective-permute-start.7
  69.1 0.7 collective-permute-start.6
  69.8 1.3 shard_map.102
  71.0 12.3 %all_to_all.30.args_0_ = f32[8,16,8,128]{3,2,1,0:T(8,128)} all-to-all(f32[8,16,8,128]{3,2,1,0:T(8,128)S(1)} %get-tuple-element.44), channel_id=1, replica_groups=mesh['sec'=4,'dev'=8] {'dev'}, dimensions={0} | all-to-all | bytes 1048576 | tf_op jit(solution)/shard_map/all_to_all | solution.py:518
  83.4 2.1 %shard_map.103 = (f32[8,5,8,128]{3,2,1,0:T(8,128)}, f32[2048,128]{1,0:T(8,128)}) custom-call(f32[8,16,8,128]{3,2,1,0:T(8,128)} %all_to_all.30.args_0_, bf16[2048,512]{1,0:T(8,128)(2,1)S(1)} %copy-done.5), custom_call_target="tpu_custom_call" | custom-call | tf_op jit(solution)/shard_map/pallas_call | solution.py:523
  85.4 1.3 collective-permute-start.8
  86.7 12.3 %all_to_all.31 = f32[8,5,8,128]{3,2,1,0:T(8,128)S(1)} all-to-all(f32[8,5,8,128]{3,2,1,0:T(8,128)} %get-tuple-element.46), channel_id=1, replica_groups=mesh['sec'=4,'dev'=8] {'dev'}, dimensions={0} | all-to-all | bytes 327680 | tf_op jit(solution)/shard_map/all_to_all | solution.py:538
  99.0 1.4 collective-permute-start.11
  100.4 1.3 collective-permute-start.10
  101.7 1.3 collective-permute-start.9
  103.0 30.9 %collective-permute-done.8.rest_0_ = f32[2048,128]{1,0:T(8,128)} collective-permute-done((f32[2048,128]{1,0:T(8,128)}, f32[2048,128]{1,0:T(8,128)}, u32[]{:S(2)}, u32[]{:S(2)}) %collective-permute-start.8) | collective-permute-done | bytes 1048608 | tf_op jit(solution)/shard_map/ppermute | solution.py:540
  133.9 2.6 %add.11 = f32[2048,128]{1,0:T(8,128)} add(f32[2048,128]{1,0:T(8,128)} %get-tuple-element.45, f32[2048,128]{1,0:T(8,128)} %collective-permute-done.8.rest_0_) | non-fusion elementwise | flops 262144 | bytes 3145728 | tf_op jit(solution)/shard_map/add | solution.py:541
  136.5 9.2 %collective-permute-done.11 = f32[5,8,128]{2,1,0:T(8,128)S(1)} collective-permute-done((f32[5,8,128]{2,1,0:T(8,128)S(1)}, f32[5,8,128]{2,1,0:T(8,128)S(1)}, u32[]{:S(2)}, u32[]{:S(2)}) %collective-permute-start.11) | collective-permute-done | bytes 20512 | tf_op jit(solution)/shard_map/ppermute | solution.py:536
  145.7 1.3 collective-permute-start.12
  147.0 8.9 %conditional.3 = (f32[40,8,128]{2,1,0:T(8,128)S(1)}) conditional(s32[]{:T(128)} %convert_element_type.22, () %tuple.24, (f32[5,8,128]{2,1,0:T(8,128)S(1)}, f32[5,8,128]{2,1,0:T(8,128)S(1)}, f32[5,8,128]{2,1,0:T(8,128)S(1)}) %tuple.28), branch_computations={%region_4.5_spmd, %region_5.6_spmd} | conditional | flops 10240 | bytes 593928 | solution.py:549
  147.1 8.8 %all_to_all.29 = f32[8,5,8,128]{3,2,1,0:T(8,128)S(1)} all-to-all(f32[8,5,8,128]{3,2,1,0:T(8,128)S(1)} %broadcast_in_dim.10), channel_id=1, replica_groups=mesh['sec'=4,'dev'=8] {'dev'}, dimensions={0} | all-to-all | bytes 327680 | tf_op jit(solution)/shard_map/cond/branch_1_fun/all_to_all | solution.py:547
  155.9 25.5 %shard_map.104 = (f32[512,512]{1,0:T(8,128)}, f32[512,512]{1,0:T(8,128)S(1)}) custom-call(f32[40,8,128]{2,1,0:T(8,128)S(1)} %get-tuple-element.56.parts_ref, f32[64,512]{1,0:T(8,128)S(1)} %broadcast_multiply_fusion.omega_ref, f32[512,512]{1,0:T(8,128)S(1)} %copy-done.7), custom_call_target="tpu_custom_call" | custom-call | tf_op jit(solution)/shard_map/pallas_call | solution.py:554
  181.4 1.0 copy-done.1
  182.4 8.0 %shard_map.105 = bf16[2048,512]{1,0:T(8,128)(2,1)} custom-call(f32[512,512]{1,0:T(8,128)} %copy-done.1, f32[64,512]{1,0:T(8,128)} %copy-done, bf16[2048,512]{1,0:T(8,128)(2,1)S(1)} %copy-done.5, f32[2048,128]{1,0:T(8,128)} %collective-permute-done.8.rest_0_, f32[2048,128]{1,0:T(8,128)} %collective-permute-done.12.rest_1_), custom_call_target="tpu_custom_call" | custom-call | tf_op jit(solution)/shard_map/pallas_call | solution.py:563
  (43 shorter events, 2.9 us)
Async XLA Ops:
  1.4 46.4 %copy-start.2 = (f32[8,32,128]{2,1,0:T(8,128)S(1)}, f32[8,32,128]{2,1,0:T(8,128)}, u32[]{:S(2)}) copy-start(f32[8,32,128]{2,1,0:T(8,128)} %u_ref.1) | copy-start | bytes 393220
  1.4 46.4 %copy-start.3 = (f32[8,32,128]{2,1,0:T(8,128)S(1)}, f32[8,32,128]{2,1,0:T(8,128)}, u32[]{:S(2)}) copy-start(f32[8,32,128]{2,1,0:T(8,128)} %e_ref.1) | copy-start | bytes 393220
  1.4 46.4 %copy-start.4 = (f32[8,32,128]{2,1,0:T(8,128)S(1)}, f32[8,32,128]{2,1,0:T(8,128)}, u32[]{:S(2)}) copy-start(f32[8,32,128]{2,1,0:T(8,128)} %k_ref.1) | copy-start | bytes 393220
  1.4 51.2 %copy-start.8 = (f32[64,512]{1,0:T(8,128)S(1)}, f32[64,512]{1,0:T(8,128)}, u32[]{:S(2)}) copy-start(f32[64,512]{1,0:T(8,128)} %param.16) | copy-start | bytes 393220
  1.4 51.2 %copy-start.9 = (f32[64]{0:T(128)S(1)}, f32[64]{0:T(128)}, u32[]{:S(2)}) copy-start(f32[64]{0:T(128)} %constant.20.clone) | copy-start | bytes 772
  47.8 19.8 %copy-start.6 = (f32[512,512]{1,0:T(8,128)}, f32[512,512]{1,0:T(8,128)S(1)}, u32[]{:S(2)}) copy-start(f32[512,512]{1,0:T(8,128)S(1)} %get-tuple-element.55.s_ref) | copy-start | bytes 3145732
  48.9 13.2 %all-to-all-start.3 = ((f32[8,104,128]{2,1,0:T(8,128)}), f32[8,104,128]{2,1,0:T(8,128)S(1)}, u32[]{:S(2)}, u32[]{:S(2)}) async-start(f32[8,104,128]{2,1,0:T(8,128)} %shard_map.98), calls=%async_computation.3 | async-start | bytes 851968 | tf_op jit(solution)/shard_map/all_to_all | solution.py:485
  52.7 103.2 %copy-start = (f32[64,512]{1,0:T(8,128)}, f32[64,512]{1,0:T(8,128)S(1)}, u32[]{:S(2)}) copy-start(f32[64,512]{1,0:T(8,128)S(1)} %broadcast_multiply_fusion.omega_ref) | copy-start | bytes 393220
  62.1 1.4 collective-permute-start.1
  62.8 0.7 collective-permute-start
  64.2 1.4 collective-permute-start.3
  64.9 0.7 collective-permute-start.2
  66.2 1.4 collective-permute-start.5
  66.9 0.7 collective-permute-start.4
  68.2 15.1 %copy-start.5 = (bf16[2048,512]{1,0:T(8,128)(2,1)S(1)}, bf16[2048,512]{1,0:T(8,128)(2,1)}, u32[]{:S(2)}) copy-start(bf16[2048,512]{1,0:T(8,128)(2,1)} %s_ref.1) | copy-start | bytes 6291460
  68.2 1.5 collective-permute-start.7
  69.1 0.7 collective-permute-start.6
  85.4 48.5 %collective-permute-start.8 = (f32[2048,128]{1,0:T(8,128)}, f32[2048,128]{1,0:T(8,128)}, u32[]{:S(2)}, u32[]{:S(2)}) collective-permute-start(f32[2048,128]{1,0:T(8,128)} %get-tuple-element.45), channel_id=1, source_target_pairs={{0,8},{16,24},{1,9},{17,25},{2,10},{18,26},{3,11},{19,27},{4,12},{... | collective-permute-start | bytes 3145736 | tf_op jit(solution)/shard_map/ppermute | solution.py:540
  99.0 56.9 %copy-start.7 = (f32[512,512]{1,0:T(8,128)S(1)}, f32[512,512]{1,0:T(8,128)}, u32[]{:S(2)}) copy-start(f32[512,512]{1,0:T(8,128)} %copy-done.6) | copy-start | bytes 3145732
  99.0 46.7 %collective-permute-start.11 = (f32[5,8,128]{2,1,0:T(8,128)S(1)}, f32[5,8,128]{2,1,0:T(8,128)S(1)}, u32[]{:S(2)}, u32[]{:S(2)}) collective-permute-start(f32[5,8,128]{2,1,0:T(8,128)S(1)} %reduce_sum.18), channel_id=1, source_target_pairs={{16,24},{17,25},{18,26},{19,27},{20,28},{21,29},{22,30},{23,31}} | collective-permute-start | bytes 61448 | tf_op jit(solution)/shard_map/ppermute | solution.py:536
  100.4 45.3 %collective-permute-start.10 = (f32[5,8,128]{2,1,0:T(8,128)S(1)}, f32[5,8,128]{2,1,0:T(8,128)S(1)}, u32[]{:S(2)}, u32[]{:S(2)}) collective-permute-start(f32[5,8,128]{2,1,0:T(8,128)S(1)} %reduce_sum.18), channel_id=1, source_target_pairs={{8,24},{9,25},{10,26},{11,27},{12,28},{13,29},{14,30},{15,31}} | collective-permute-start | bytes 61448 | tf_op jit(solution)/shard_map/ppermute | solution.py:536
  101.7 44.0 %collective-permute-start.9 = (f32[5,8,128]{2,1,0:T(8,128)S(1)}, f32[5,8,128]{2,1,0:T(8,128)S(1)}, u32[]{:S(2)}, u32[]{:S(2)}) collective-permute-start(f32[5,8,128]{2,1,0:T(8,128)S(1)} %reduce_sum.18), channel_id=1, source_target_pairs={{0,24},{1,25},{2,26},{3,27},{4,28},{5,29},{6,30},{7,31}} | collective-permute-start | bytes 61448 | tf_op jit(solution)/shard_map/ppermute | solution.py:536
  145.7 36.6 %collective-permute-start.12 = (f32[2048,128]{1,0:T(8,128)}, f32[2048,128]{1,0:T(8,128)}, u32[]{:S(2)}, u32[]{:S(2)}) collective-permute-start(f32[2048,128]{1,0:T(8,128)} %add.11), channel_id=1, source_target_pairs={{8,24},{9,25},{10,26},{11,27},{12,28},{13,29},{14,30},{15,31}} | collective-permute-start | bytes 3145736 | tf_op jit(solution)/shard_map/ppermute | solution.py:543
  181.4 1.0 copy-start.1
where the time goes:
time: 191 us; the launch traced here: 190 us
  blocking collectives  76 us (40%)
  waiting for transfers between devices  49.5 us (26%)
  Pallas kernels  39.7 us (21%)
  starting transfers between devices  15.9 us (8%)
  matrix products  3.59 us (2%)
  other arithmetic  3.54 us (2%)
    all_to_all x2, blocking collectives, whole_gram(): own = lax.all_to_all(own, 'dev', split_axis=0, concat_axis=0, tiled=True)  42.5 us
    ppermute x1, waiting for transfers between devices, shards(): lax.ppermute(wide, 'sec', [(i, i + 1) for i in range(0, sections - 1, 2)])  30.9 us
    pallas_call x1, Pallas kernels, shards(): pl.pallas_call(functools.partial(factor_kernel, scale, sections), out_sha...  25.5 us
    all_to_all x1, blocking collectives, shards(): lax.all_to_all(moved, 'dev', split_axis=0, concat_axis=0, tiled=True)  12.3 us
    all_to_all x1, blocking collectives, shards(): lax.all_to_all(parts, 'dev', split_axis=0, concat_axis=0, tiled=True)  12.3 us
    all_to_all x1, waiting for transfers between devices, shards(): lax.all_to_all(outgoing, 'dev', split_axis=0, concat_axis=0, tiled=True)  9.37 us
    ppermute x3, waiting for transfers between devices, to_analysis(): lax.ppermute(x, 'sec', [(i, sections - 1)])  9.19 us
    all_to_all x1, blocking collectives, exchange(): return lax.all_to_all(total, 'dev', split_axis=0, concat_axis=0, tiled=True)  8.81 us
  transfers between devices with their start and end apart: 14, of which 3 were waited for; matrix products, arithmetic and copies ran while one was open for 1% of the time, Pallas kernels for 13%

commit v1 on v0

--- a/solution.py
+++ b/solution.py
@@ -243,7 +243,12 @@
     return x1, x2, (rest - x2.astype(jnp.float32)).astype(jnp.bfloat16)
 
 
-def factor_block(d, e, sub, lane):
+def reciprocal(x):
+    guess = pl.reciprocal(x, approx=True)
+    return guess * (2.0 - x * guess)
+
+
+def factor_block(d, e, sub, lane, spread):
     tiles = len(d)
 
     def wide(x):
@@ -258,21 +263,36 @@
     for p in range(tiles):
         first = 8 * p
         cols = [wide(d[p][:, first + j : first + j + 1]) for j in range(8)]
-        s = [[wide(cols[k][j : j + 1, :]) if k >= j else None for k in range(8)] for j in range(8)]
-        t = [wide(d[p][j : j + 1, :]) for j in range(8)]
-        te = [wide(e[p][j : j + 1, :]) for j in range(8)]
+        base = 80 * (p % 2)
+        for k, value in enumerate(cols + [d[p], e[p]]):
+            spread[base + 8 * k : base + 8 * k + 8, :] = value
+
+        def row(k, j, base=base):
+            return spread[pl.ds(base + 8 * k + j, 8, stride=0), :]
+
+        s = [[row(k, j) if k >= j else None for k in range(8)] for j in range(8)]
+        t = [row(8, j) for j in range(8)]
+        te = [row(9, j) for j in range(8)]
         inv, m = [], [[None] * 8 for _ in range(8)]
-        for j in range(8):
-            guess = pl.reciprocal(s[j][j], approx=True)
-            guess = guess * (2.0 - s[j][j] * guess)
-            inv.append(guess * (2.0 - s[j][j] * guess))
-            for k in range(j + 1, 8):
-                m[j][k] = s[j][k] * inv[j]
-            for k in range(j + 1, 8):
-                for n in range(k, 8):
-                    s[k][n] = s[k][n] - m[j][k] * s[j][n]
-                t[k] = t[k] - m[j][k] * t[j]
-                te[k] = te[k] - m[j][k] * te[j]
+        for j in range(0, 8, 2):
+            n = j + 1
+            a, b, c = s[j][j], s[j][n], s[n][n]
+            det = a * c - b * b
+            inv_a, inv_det = reciprocal(a), reciprocal(det)
+            inv += [inv_a, a * inv_det]
+            m[j][n] = b * inv_a
+            s[n][n] = det * inv_a
+            t[n] = t[n] - m[j][n] * t[j]
+            te[n] = te[n] - m[j][n] * te[j]
+            for k in range(j + 2, 8):
+                m[j][k] = s[j][k] * inv_a
+                m[n][k] = (a * s[n][k] - b * s[j][k]) * inv_det
+                s[n][k] = s[n][k] - m[j][n] * s[j][k]
+            for k in range(j + 2, 8):
+                for i in range(k, 8):
+                    s[k][i] = (s[k][i] - m[j][k] * s[j][i]) - m[n][k] * s[n][i]
+                t[k] = (t[k] - m[j][k] * t[j]) - m[n][k] * t[n]
+                te[k] = (te[k] - m[j][k] * te[j]) - m[n][k] * te[n]
         if p + 1 < tiles:
             z, ze = [None] * 8, [None] * 8
             for j in reversed(range(8)):
@@ -308,19 +328,19 @@
     return jnp.concatenate(d, axis=0), jnp.concatenate(e, axis=0)
 
 
-def factor_kernel(scale, sections, parts_ref, omega_ref, s_ref, factor_ref, inverse_ref, g):
+def factor_kernel(scale, sections, parts_ref, omega_ref, s_ref, factor_ref, inverse_ref, g, spread):
     analysis = lax.axis_index("sec") == sections - 1
 
     @pl.when(analysis)
     def _():
-        factorize(scale, parts_ref, omega_ref, s_ref, factor_ref, inverse_ref, g)
+        factorize(scale, parts_ref, omega_ref, s_ref, factor_ref, inverse_ref, g, spread)
 
     @pl.when(jnp.logical_not(analysis))
     def _():
         factor_ref[...] = jnp.zeros(factor_ref.shape, jnp.float32)
 
 
-def factorize(scale, parts_ref, omega_ref, s_ref, factor_ref, inverse_ref, g):
+def factorize(scale, parts_ref, omega_ref, s_ref, factor_ref, inverse_ref, g, spread):
     rank = s_ref.shape[0]
     snaps = omega_ref.shape[0]
     strips = rank // LANES
@@ -356,7 +376,7 @@
         start = pl.multiple_of(k * LANES, LANES)
         d = [g[pl.ds(start + 8 * i, 8), pl.ds(start, LANES)] for i in range(tiles)]
         e = [jnp.where(lane == sub + 8 * i, 1.0, 0.0) for i in range(tiles)]
-        upper, small = factor_block(d, e, sub, lane)
+        upper, small = factor_block(d, e, sub, lane, spread)
         factor_ref[pl.ds(start, LANES), pl.ds(start, LANES)] = upper
         inverse_ref[pl.ds(start, LANES), pl.ds(start, LANES)] = small
         for at in range(strips):
@@ -414,7 +434,8 @@
         )
         x1, x2 = split(inverse)
         m1, m2 = split(jnp.concatenate([mixed, mixed], axis=0))
-        rows = 512
+        stack = jnp.concatenate([x1, x2, m1, m2], axis=0)
+        rows = 1024
 
         def strip(i, carry):
             at = pl.ds(pl.multiple_of(i * rows, rows), rows)
@@ -423,7 +444,7 @@
             for piece in pieces[1:]:
                 w = w + piece[at, :]
             w = w.astype(jnp.bfloat16)
-            q = (dot(s, x1) + dot(s, x2)) + (dot(w, m1) + dot(w, m2))
+            q = dot(jnp.concatenate([s, s, w, w], axis=1), stack)
             out_ref[at, :] = q.astype(jnp.bfloat16)
             return carry
 
@@ -536,11 +557,10 @@
         return [lax.ppermute(x, "sec", [(i, sections - 1)]) for i in range(sections - 1)]
 
     terms = lax.all_to_all(parts, "dev", split_axis=0, concat_axis=0, tiled=True)
-    terms = to_analysis(jnp.sum(terms, axis=0))
-    hop = lax.ppermute(wide, "sec", [(i, i + 1) for i in range(0, sections - 1, 2)])
-    merged, terms = lax.optimization_barrier((wide + hop, terms))
-    pieces = [hop]
-    pieces += [lax.ppermute(merged, "sec", [(i, sections - 1)]) for i in range(1, sections - 1, 2)]
+    total = jnp.sum(terms, axis=0)
+    terms = to_analysis(total)
+    wide, *terms = lax.optimization_barrier((wide, *terms))
+    pieces = to_analysis(wide)
 
     def exchange(terms):
         total = jnp.broadcast_to(sum(terms[1:], terms[0])[None], parts.shape)
@@ -556,7 +576,7 @@
         out_shape=(jax.ShapeDtypeStruct((rank, rank), f32),) * 2,
         in_specs=vmem(*operands),
         out_specs=tuple(vmem(0, 0)),
-        scratch_shapes=[pltpu.VMEM((rank, rank), f32)],
+        scratch_shapes=[pltpu.VMEM((rank, rank), f32), pltpu.VMEM((160, LANES), f32)],
         compiler_params=big(),
     )(*operands)
     operands = (inverse, scaled, sketch_in, *pieces)

time: 191 us -> 185 us (0.969)
  Pallas kernels: 39.7 us -> 33.4 us
  other arithmetic: 3.54 us -> 0.93 us
  waiting for transfers between devices: 49.5 us -> 52 us
    ppermute x3 -> x6, waiting for transfers between devices: 9.19 us -> 42.6 us  [to_analysis(): lax.ppermute(x, 'sec', [(i, sections - 1)])]
    ppermute x2 -> x0, waiting for transfers between devices: 30.9 us -> none  [the longest x1 30.9 us: shards(): lax.ppermute(wide, 'sec', [(i, i + 1) for i in range(0, sections - 1, 2)])]
    pallas_call x1, Pallas kernels: 25.5 us -> 19.6 us  [shards(): pl.pallas_call(functools.partial(factor_kernel, scale, sections), out_sha...]
    ppermute x3 -> x6, starting transfers between devices: 4.01 us -> 7.74 us  [to_analysis(): lax.ppermute(x, 'sec', [(i, sections - 1)])]
    add x1 -> x0, other arithmetic: 2.61 us -> none  [shards(): merged, terms = lax.optimization_barrier((wide + hop, terms))]
    ppermute x2 -> x0, starting transfers between devices: 2.56 us -> none  [the longest x1 1.28 us: shards(): lax.ppermute(merged, 'sec', [(i, sections - 1)])]
  transfers between devices with their start and end apart: 14 -> 15, of which waited for: 3 -> 2; matrix products, arithmetic and copies ran while one was open for 1% -> 0% of each run, Pallas kernels for 13% -> 11%
where the time goes in v1:
time: 185 us; the launch traced here: 184 us
  blocking collectives  75 us (41%)
  waiting for transfers between devices  52 us (28%)
  Pallas kernels  33.4 us (18%)
  starting transfers between devices  17 us (9%)
  matrix products  3.59 us (2%)
    ppermute x6, waiting for transfers between devices, to_analysis(): lax.ppermute(x, 'sec', [(i, sections - 1)])  42.6 us
    all_to_all x2, blocking collectives, whole_gram(): own = lax.all_to_all(own, 'dev', split_axis=0, concat_axis=0, tiled=True)  42.5 us
    pallas_call x1, Pallas kernels, shards(): pl.pallas_call(functools.partial(factor_kernel, scale, sections), out_sha...  19.6 us
    all_to_all x1, blocking collectives, shards(): lax.all_to_all(moved, 'dev', split_axis=0, concat_axis=0, tiled=True)  12.3 us
    all_to_all x1, blocking collectives, shards(): lax.all_to_all(parts, 'dev', split_axis=0, concat_axis=0, tiled=True)  11.3 us
    all_to_all x1, waiting for transfers between devices, shards(): lax.all_to_all(outgoing, 'dev', split_axis=0, concat_axis=0, tiled=True)  9.37 us
    all_to_all x1, blocking collectives, exchange(): return lax.all_to_all(total, 'dev', split_axis=0, concat_axis=0, tiled=True)  8.81 us
    ppermute x6, starting transfers between devices, to_analysis(): lax.ppermute(x, 'sec', [(i, sections - 1)])  7.74 us
  transfers between devices with their start and end apart: 15, of which 2 were waited for; matrix products, arithmetic and copies ran while one was open for 0% of the time, Pallas kernels for 11%

profile of v1, /device:TPU:5, one launch (start us, length us, event | category | flops | bytes accessed | tf_op | source)
XLA Modules:
  0.0 184.2 jit_solution(17434271532239793943)
XLA Ops:
  0.6 0.7 add_convert_fusion
  1.4 46.4 %conditional.2 = (f32[512,512]{1,0:T(8,128)S(1)}) conditional(s32[]{:T(128)} %convert_element_type.22, () %tuple.25, bf16[2048,512]{1,0:T(8,128)(2,1)} %s_ref.1), branch_computations={%region_0.1_spmd, %region_1.3_spmd} | conditional | flops 1073971200 | bytes 9699340 | solution.py:508
  1.5 3.6 %fusion = f32[512,512]{1,0:T(8,128)S(1)} fusion(bf16[2048,512]{1,0:T(8,128)(2,1)} %param.1), kind=kOutput, calls=%fused_computation.4 | convolution fusion | flops 1073741824 | bytes 3145728 | tf_op jit(solution)/shard_map/cond/branch_1_fun/dot_general | solution.py:480
  5.1 24.8 %all_to_all.27 = f32[8,64,512]{2,1,0:T(8,128)S(1)} all-to-all(f32[8,64,512]{2,1,0:T(8,128)S(1)} %bitcast.14), channel_id=1, replica_groups=mesh['sec'=4,'dev'=8] {'dev'}, dimensions={0} | all-to-all | bytes 2097152 | tf_op jit(solution)/shard_map/cond/branch_1_fun/all_to_all | solution.py:484
  30.1 17.7 %all_to_all.28 = f32[8,64,512]{2,1,0:T(8,128)S(1)} all-to-all(f32[8,64,512]{2,1,0:T(8,128)S(1)} %broadcast_in_dim.5), channel_id=1, replica_groups=mesh['sec'=4,'dev'=8] {'dev'}, dimensions={0} | all-to-all | bytes 2097152 | tf_op jit(solution)/shard_map/cond/branch_1_fun/all_to_all | solution.py:486
  47.8 1.1 shard_map.98
  48.9 3.7 %all-to-all-start.3 = ((f32[8,104,128]{2,1,0:T(8,128)}), f32[8,104,128]{2,1,0:T(8,128)S(1)}, u32[]{:S(2)}, u32[]{:S(2)}) async-start(f32[8,104,128]{2,1,0:T(8,128)} %shard_map.98), calls=%async_computation.3 | async-start | bytes 851968 | tf_op jit(solution)/shard_map/all_to_all | solution.py:506
  52.8 9.4 %all-to-all-done.3.args_2_.args_5_ = f32[8,104,128]{2,1,0:T(8,128)S(1)} async-done(((f32[8,104,128]{2,1,0:T(8,128)}), f32[8,104,128]{2,1,0:T(8,128)S(1)}, u32[]{:S(2)}, u32[]{:S(2)}) %all-to-all-start.3) | async-done | bytes 426016 | tf_op jit(solution)/shard_map/all_to_all | solution.py:506
  62.1 0.7 collective-permute-start.1
  62.8 0.7 collective-permute-start
  64.2 0.7 collective-permute-start.3
  64.9 0.7 collective-permute-start.2
  66.2 0.7 collective-permute-start.5
  66.9 0.7 collective-permute-start.4
  68.2 0.8 collective-permute-start.7
  69.1 0.7 collective-permute-start.6
  69.8 1.3 shard_map.102
  71.0 12.3 %all_to_all.30.args_0_ = f32[8,16,8,128]{3,2,1,0:T(8,128)} all-to-all(f32[8,16,8,128]{3,2,1,0:T(8,128)S(1)} %get-tuple-element.44), channel_id=1, replica_groups=mesh['sec'=4,'dev'=8] {'dev'}, dimensions={0} | all-to-all | bytes 1048576 | tf_op jit(solution)/shard_map/all_to_all | solution.py:539
  83.4 2.2 %shard_map.103 = (f32[8,5,8,128]{3,2,1,0:T(8,128)}, f32[2048,128]{1,0:T(8,128)}) custom-call(f32[8,16,8,128]{3,2,1,0:T(8,128)} %all_to_all.30.args_0_, bf16[2048,512]{1,0:T(8,128)(2,1)S(1)} %copy-done.5), custom_call_target="tpu_custom_call" | custom-call | tf_op jit(solution)/shard_map/pallas_call | solution.py:544
  85.5 11.3 %all_to_all.31 = f32[8,5,8,128]{3,2,1,0:T(8,128)S(1)} all-to-all(f32[8,5,8,128]{3,2,1,0:T(8,128)} %get-tuple-element.46), channel_id=1, replica_groups=mesh['sec'=4,'dev'=8] {'dev'}, dimensions={0} | all-to-all | bytes 327680 | tf_op jit(solution)/shard_map/all_to_all | solution.py:559
  96.9 1.3 collective-permute-start.10
  98.2 1.3 collective-permute-start.9
  99.5 1.3 collective-permute-start.8
  100.8 42.6 %collective-permute-done.10 = f32[5,8,128]{2,1,0:T(8,128)S(1)} collective-permute-done((f32[5,8,128]{2,1,0:T(8,128)S(1)}, f32[5,8,128]{2,1,0:T(8,128)S(1)}, u32[]{:S(2)}, u32[]{:S(2)}) %collective-permute-start.10) | collective-permute-done | bytes 20512 | tf_op jit(solution)/shard_map/ppermute | solution.py:557
  143.4 1.3 collective-permute-start.13
  144.7 1.3 collective-permute-start.12
  146.0 1.3 collective-permute-start.11
  147.3 8.9 %conditional.3 = (f32[40,8,128]{2,1,0:T(8,128)S(1)}) conditional(s32[]{:T(128)} %convert_element_type.22, () %tuple.24, (f32[5,8,128]{2,1,0:T(8,128)S(1)}, f32[5,8,128]{2,1,0:T(8,128)S(1)}, f32[5,8,128]{2,1,0:T(8,128)S(1)}) %tuple.28), branch_computations={%region_4.5_spmd, %region_5.6_spmd} | conditional | flops 10240 | bytes 593928 | solution.py:569
  147.3 8.8 %all_to_all.29 = f32[8,5,8,128]{3,2,1,0:T(8,128)S(1)} all-to-all(f32[8,5,8,128]{3,2,1,0:T(8,128)S(1)} %broadcast_in_dim.10), channel_id=1, replica_groups=mesh['sec'=4,'dev'=8] {'dev'}, dimensions={0} | all-to-all | bytes 327680 | tf_op jit(solution)/shard_map/cond/branch_1_fun/all_to_all | solution.py:567
  156.2 19.6 %shard_map.104 = (f32[512,512]{1,0:T(8,128)}, f32[512,512]{1,0:T(8,128)S(1)}) custom-call(f32[40,8,128]{2,1,0:T(8,128)S(1)} %get-tuple-element.56.parts_ref, f32[64,512]{1,0:T(8,128)S(1)} %broadcast_multiply_fusion.omega_ref, f32[512,512]{1,0:T(8,128)S(1)} %copy-done.7), custom_call_target="tpu_custom_call" | custom-call | tf_op jit(solution)/shard_map/pallas_call | solution.py:574
  175.8 1.0 copy-done.1
  176.8 7.4 %shard_map.105 = bf16[2048,512]{1,0:T(8,128)(2,1)} custom-call(f32[512,512]{1,0:T(8,128)} %copy-done.1, f32[64,512]{1,0:T(8,128)} %copy-done, bf16[2048,512]{1,0:T(8,128)(2,1)S(1)} %copy-done.5, f32[2048,128]{1,0:T(8,128)} %collective-permute-done.11.rest_0_, f32[2048,128]{1,0:T(8,128)} %collective-permute-done.12.rest_1_, ...), custom_call_target="tpu_custom_call" | custom-call | tf_op jit(solution)/shard_map/pallas_call | solution.py:583
  (44 shorter events, 2.3 us)
Async XLA Ops:
  1.4 46.4 %copy-start.2 = (f32[8,32,128]{2,1,0:T(8,128)S(1)}, f32[8,32,128]{2,1,0:T(8,128)}, u32[]{:S(2)}) copy-start(f32[8,32,128]{2,1,0:T(8,128)} %u_ref.1) | copy-start | bytes 393220
  1.4 46.4 %copy-start.3 = (f32[8,32,128]{2,1,0:T(8,128)S(1)}, f32[8,32,128]{2,1,0:T(8,128)}, u32[]{:S(2)}) copy-start(f32[8,32,128]{2,1,0:T(8,128)} %e_ref.1) | copy-start | bytes 393220
  1.4 46.4 %copy-start.4 = (f32[8,32,128]{2,1,0:T(8,128)S(1)}, f32[8,32,128]{2,1,0:T(8,128)}, u32[]{:S(2)}) copy-start(f32[8,32,128]{2,1,0:T(8,128)} %k_ref.1) | copy-start | bytes 393220
  1.4 51.2 %copy-start.8 = (f32[64,512]{1,0:T(8,128)S(1)}, f32[64,512]{1,0:T(8,128)}, u32[]{:S(2)}) copy-start(f32[64,512]{1,0:T(8,128)} %param.16) | copy-start | bytes 393220
  1.4 51.2 %copy-start.9 = (f32[64]{0:T(128)S(1)}, f32[64]{0:T(128)}, u32[]{:S(2)}) copy-start(f32[64]{0:T(128)} %constant.20.clone) | copy-start | bytes 772
  47.8 15.7 %copy-start.6 = (f32[512,512]{1,0:T(8,128)}, f32[512,512]{1,0:T(8,128)S(1)}, u32[]{:S(2)}) copy-start(f32[512,512]{1,0:T(8,128)S(1)} %get-tuple-element.55.s_ref) | copy-start | bytes 3145732
  48.9 13.2 %all-to-all-start.3 = ((f32[8,104,128]{2,1,0:T(8,128)}), f32[8,104,128]{2,1,0:T(8,128)S(1)}, u32[]{:S(2)}, u32[]{:S(2)}) async-start(f32[8,104,128]{2,1,0:T(8,128)} %shard_map.98), calls=%async_computation.3 | async-start | bytes 851968 | tf_op jit(solution)/shard_map/all_to_all | solution.py:506
  52.7 103.4 %copy-start = (f32[64,512]{1,0:T(8,128)}, f32[64,512]{1,0:T(8,128)S(1)}, u32[]{:S(2)}) copy-start(f32[64,512]{1,0:T(8,128)S(1)} %broadcast_multiply_fusion.omega_ref) | copy-start | bytes 393220
  62.1 1.4 collective-permute-start.1
  62.8 0.7 collective-permute-start
  64.2 1.4 collective-permute-start.3
  64.9 0.7 collective-permute-start.2
  66.2 1.4 collective-permute-start.5
  66.9 0.7 collective-permute-start.4
  68.2 15.1 %copy-start.5 = (bf16[2048,512]{1,0:T(8,128)(2,1)S(1)}, bf16[2048,512]{1,0:T(8,128)(2,1)}, u32[]{:S(2)}) copy-start(bf16[2048,512]{1,0:T(8,128)(2,1)} %s_ref.1) | copy-start | bytes 6291460
  68.2 1.5 collective-permute-start.7
  69.1 0.7 collective-permute-start.6
  83.4 72.8 %copy-start.7 = (f32[512,512]{1,0:T(8,128)S(1)}, f32[512,512]{1,0:T(8,128)}, u32[]{:S(2)}) copy-start(f32[512,512]{1,0:T(8,128)} %copy-done.6) | copy-start | bytes 3145732
  96.9 46.5 %collective-permute-start.10 = (f32[5,8,128]{2,1,0:T(8,128)S(1)}, f32[5,8,128]{2,1,0:T(8,128)S(1)}, u32[]{:S(2)}, u32[]{:S(2)}) collective-permute-start(f32[5,8,128]{2,1,0:T(8,128)S(1)} %reduce_sum.18), channel_id=1, source_target_pairs={{16,24},{17,25},{18,26},{19,27},{20,28},{21,29},{22,30},{23,31}} | collective-permute-start | bytes 61448 | tf_op jit(solution)/shard_map/ppermute | solution.py:557
  98.2 45.2 %collective-permute-start.9 = (f32[5,8,128]{2,1,0:T(8,128)S(1)}, f32[5,8,128]{2,1,0:T(8,128)S(1)}, u32[]{:S(2)}, u32[]{:S(2)}) collective-permute-start(f32[5,8,128]{2,1,0:T(8,128)S(1)} %reduce_sum.18), channel_id=1, source_target_pairs={{8,24},{9,25},{10,26},{11,27},{12,28},{13,29},{14,30},{15,31}} | collective-permute-start | bytes 61448 | tf_op jit(solution)/shard_map/ppermute | solution.py:557
  99.5 43.9 %collective-permute-start.8 = (f32[5,8,128]{2,1,0:T(8,128)S(1)}, f32[5,8,128]{2,1,0:T(8,128)S(1)}, u32[]{:S(2)}, u32[]{:S(2)}) collective-permute-start(f32[5,8,128]{2,1,0:T(8,128)S(1)} %reduce_sum.18), channel_id=1, source_target_pairs={{0,24},{1,25},{2,26},{3,27},{4,28},{5,29},{6,30},{7,31}} | collective-permute-start | bytes 61448 | tf_op jit(solution)/shard_map/ppermute | solution.py:557
  143.4 33.4 %collective-permute-start.13 = (f32[2048,128]{1,0:T(8,128)}, f32[2048,128]{1,0:T(8,128)}, u32[]{:S(2)}, u32[]{:S(2)}) collective-permute-start(f32[2048,128]{1,0:T(8,128)} %get-tuple-element.53), channel_id=1, source_target_pairs={{16,24},{17,25},{18,26},{19,27},{20,28},{21,29},{22,30},{23,31}} | collective-permute-start | bytes 3145736 | tf_op jit(solution)/shard_map/ppermute | solution.py:557
  144.7 32.1 %collective-permute-start.12 = (f32[2048,128]{1,0:T(8,128)}, f32[2048,128]{1,0:T(8,128)}, u32[]{:S(2)}, u32[]{:S(2)}) collective-permute-start(f32[2048,128]{1,0:T(8,128)} %get-tuple-element.53), channel_id=1, source_target_pairs={{8,24},{9,25},{10,26},{11,27},{12,28},{13,29},{14,30},{15,31}} | collective-permute-start | bytes 3145736 | tf_op jit(solution)/shard_map/ppermute | solution.py:557
  146.0 30.8 %collective-permute-start.11 = (f32[2048,128]{1,0:T(8,128)}, f32[2048,128]{1,0:T(8,128)}, u32[]{:S(2)}, u32[]{:S(2)}) collective-permute-start(f32[2048,128]{1,0:T(8,128)} %get-tuple-element.53), channel_id=1, source_target_pairs={{0,24},{1,25},{2,26},{3,27},{4,28},{5,29},{6,30},{7,31}} | collective-permute-start | bytes 3145736 | tf_op jit(solution)/shard_map/ppermute | solution.py:557
  175.8 1.0 copy-start.1
